TPU v7x, 256 devices: a whole 4x4x8 slice. The times are simulated.
256 devices in a mesh: dp: 16 (over z, core), expert: 16 (over y, x).
Axes of the slice: x: 4, y: 4, z: 8, core: 2. Of those that a mesh axis runs over, the one named last changes fastest.
Arguments:
- tokens: bfloat16 [65536, 1024], P(('dp', 'expert')), may hold values from -6 to 6
- cotangent: bfloat16 [65536, 1024], P(('dp', 'expert')), may hold values from -6 to 6
- route_logits: float32 [65536, 2], P(('dp', 'expert')), may hold values from -6 to 6
- expert_ids: int32 [65536, 2], P(('dp', 'expert')), may hold values from 0 to 31, as said below
- slot_pos: int32 [65536, 2], P(('dp', 'expert')), may hold values from 0 to 31, as said below
- w_in: bfloat16 [32, 1024, 1536], P('expert'), may hold values from -0.1875 to 0.1875
- w_down: bfloat16 [32, 768, 1024], P('expert'), may hold values from -0.21875 to 0.21875
Outputs:
- input_grad: bfloat16 [65536, 1024], P(('dp', 'expert'))
- grad_in: float32 [32, 1024, 1536], P('expert', 'dp')
- grad_down: float32 [32, 768, 1024], P('expert', 'dp')
Inputs may be any that keep to these rules, and one draw needn't show every extreme that they name: `expert_ids`: each row names 2 different experts. Within each aligned block of 256 rows (the tokens of one device) no expert is named more than 32 times, and one expert, the same in all blocks, is named exactly 32 times in every block. `slot_pos`: within each aligned block of 256 rows, entries whose matching expert_ids entries name the same expert are distinct.
All inputs are finite; a program needn't handle non-finite values.
Results may differ from a plain program's by a relative error of at most 0.02.
Values may be sent and summed in bfloat16 or wider, within the bound.
A program may use at most 128 MiB of HBM per device.

v0:
```python
import jax
import jax.numpy as jnp
from jax import lax
from jax.sharding import PartitionSpec as P

TOP = 2


def recompute(input_slots, w_in, hidden_width):
    gate = jnp.einsum(
        "ksd,kdf->ksf", input_slots, w_in[:, :, :hidden_width], preferred_element_type=jnp.float32
    )
    upper = jnp.einsum(
        "ksd,kdf->ksf", input_slots, w_in[:, :, hidden_width:], preferred_element_type=jnp.float32
    )
    sigmoid_gate = jax.nn.sigmoid(gate)
    activated = gate * sigmoid_gate
    hidden = (activated * upper).astype(jnp.bfloat16)
    return (gate, upper, sigmoid_gate, activated, hidden)


def per_device(tokens, cotangent, route_logits, expert_ids, slot_pos, w_in, w_down):
    token_count, width = tokens.shape
    local_experts = w_in.shape[0]
    hidden_width = w_down.shape[1]
    n_expert = lax.axis_size("expert")
    n_dp = lax.axis_size("dp")
    experts_all = local_experts * n_expert
    capacity = 2 * TOP * token_count // experts_all
    first = jax.nn.sigmoid(route_logits[:, 0] - route_logits[:, 1])
    combine = (first, 1.0 - first)
    cotangent_wide = cotangent.astype(jnp.float32)
    destination = (expert_ids * capacity + slot_pos).reshape(-1)
    target = expert_ids * (2 * capacity) + slot_pos
    buffer_row = lax.broadcasted_iota(jnp.int32, (experts_all * 2 * capacity, token_count), 0)
    picks = []
    for k in range(TOP):
        picks.append((buffer_row == target[None, :, k]).astype(jnp.bfloat16))
    token_picks = picks[0] + picks[1]
    send = jnp.dot(token_picks, tokens, preferred_element_type=jnp.float32)
    for k in range(TOP):
        scaled = (combine[k][:, None] * cotangent_wide).astype(jnp.bfloat16)
        shifted = (buffer_row == target[None, :, k] + capacity).astype(jnp.bfloat16)
        send = send + jnp.dot(shifted, scaled, preferred_element_type=jnp.float32)
    send = send.astype(jnp.bfloat16).reshape(experts_all, 2, capacity, width)
    got = lax.all_to_all(send, "expert", split_axis=0, concat_axis=0, tiled=True)
    got = got.reshape(n_expert, local_experts, 2, capacity, width)
    got = jnp.transpose(got, (2, 1, 0, 3, 4)).reshape(2, local_experts, n_expert * capacity, width)
    input_slots, cotangent_slots = (got[0], got[1])
    gate, upper, sigmoid_gate, activated, hidden = recompute(input_slots, w_in, hidden_width)
    grad_hidden = jnp.einsum(
        "ksd,kfd->ksf", cotangent_slots, w_down, preferred_element_type=jnp.float32
    )
    term_down = jnp.einsum(
        "ksf,ksd->kfd", hidden, cotangent_slots, preferred_element_type=jnp.float32
    )
    grad_gate = grad_hidden * upper * sigmoid_gate * (1.0 + gate * (1.0 - sigmoid_gate))
    grad_up = grad_hidden * activated
    grad_pair = jnp.concatenate([grad_gate, grad_up], axis=2).astype(jnp.bfloat16)
    term_in = jnp.einsum("ksd,ksf->kdf", input_slots, grad_pair, preferred_element_type=jnp.float32)
    returned = jnp.einsum(
        "ksf,kdf->ksd", grad_pair, w_in, preferred_element_type=jnp.float32
    ).astype(jnp.bfloat16)
    arrived = lax.all_to_all(returned, "expert", split_axis=1, concat_axis=0, tiled=True)
    rows = arrived.reshape(-1, width)[destination].reshape(token_count, TOP, width)
    input_grad = jnp.sum(rows.astype(jnp.float32), axis=1).astype(jnp.bfloat16)
    in_rows, in_cols = (term_in.shape[1], term_in.shape[2])
    down_rows, down_cols = (term_down.shape[1], term_down.shape[2])
    rows_q = down_rows // n_dp
    main = rows_q * down_cols // in_cols
    spare = in_cols - down_cols
    part_in = term_in.astype(jnp.bfloat16).reshape(local_experts, n_dp, in_rows // n_dp, in_cols)
    part_down = term_down.astype(jnp.bfloat16).reshape(local_experts, n_dp, rows_q, down_cols)
    pieces = [part_down[:, :, main:, c : c + spare] for c in range(0, down_cols, spare)]
    packed = jnp.concatenate([part_down[:, :, :main], jnp.concatenate(pieces, axis=2)], axis=3)
    parts = jnp.concatenate([part_in, packed], axis=2).reshape(local_experts, -1, in_cols)
    summed = lax.psum_scatter(parts, "dp", scatter_dimension=1, tiled=True)
    grad_in = summed[:, : in_rows // n_dp].astype(jnp.float32)
    got_down = summed[:, in_rows // n_dp :]
    rest = rows_q - main
    tail = [got_down[:, i * rest : (i + 1) * rest, down_cols:] for i in range(down_cols // spare)]
    grad_down = jnp.concatenate([got_down[:, :, :down_cols], jnp.concatenate(tail, axis=2)], axis=1)
    grad_down = grad_down.astype(jnp.float32)
    return (input_grad, grad_in, grad_down)


def solution(mesh):
    in_specs = (
        P(("dp", "expert"), None),
        P(("dp", "expert"), None),
        P(("dp", "expert"), None),
        P(("dp", "expert"), None),
        P(("dp", "expert"), None),
        P("expert", None, None),
        P("expert", None, None),
    )
    out_specs = (P(("dp", "expert"), None), P("expert", "dp", None), P("expert", "dp", None))
    return jax.shard_map(
        per_device, mesh=mesh, in_specs=in_specs, out_specs=out_specs, check_vma=False
    )
```

profile of v0, /device:TPU:4, one launch (start us, length us, event | category | flops | bytes accessed | tf_op | source)
XLA Modules:
  0.0 174.8 jit_solution(13041412101257724786)
XLA Ops:
  7.2 0.9 multiply_add_fusion
  8.1 2.4 %fusion.13 = f32[2048,1024]{1,0:T(8,128)S(1)} fusion(bf16[256,1024]{1,0:T(8,128)(2,1)} %param.7, s32[256]{0:T(256)S(1)} %bitcast.44, s32[256]{0:T(256)S(1)} %bitcast.42), kind=kOutput, calls=%fused_computation.30 | convolution fusion | flops 1077936128 | bytes 8914944 | tf_op jit(solution)/shard_map/dot_general | solution.py:40
  10.5 1.3 fusion.7
  11.9 2.6 %add_convert_fusion = bf16[2048,1024]{1,0:T(8,128)(2,1)S(1)} fusion(f32[2048,1024]{1,0:T(8,128)S(1)} %fusion.13, f32[2048,1024]{1,0:T(8,128)S(1)} %fusion.7, s32[256]{0:T(256)S(1)} %broadcast_add_fusion, bf16[256,1024]{1,0:T(8,128)(2,1)} %param.8, f32[256]{0:T(256)S(1)} %bitcast.46), kind=kOutput, calls=%fused_computation.2 | convolution fusion | flops 1081344000 | bytes 21497856 | tf_op jit(solution)/shard_map/dot_general | solution.py:44
  14.5 55.5 %all_to_all.20 = bf16[32,2,32,1024]{3,2,1,0:T(8,128)(2,1)S(1)} all-to-all(bf16[32,2,32,1024]{3,2,1,0:T(8,128)(2,1)S(1)} %bitcast.31), channel_id=1, replica_groups=mesh['dp'=16,'expert'=16] {'expert'}, dimensions={0} | all-to-all | bytes 8388608 | tf_op jit(solution)/shard_map/all_to_all | solution.py:46
  70.0 0.8 copy.28
  71.4 1.9 %fusion.32 = f32[2,512,768]{2,1,0:T(8,128)S(1)} fusion(bf16[2,512,1024]{2,1,0:T(8,128)(2,1)S(1)} %bitcast.39, bf16[2,768,1024]{2,1,0:T(8,128)(2,1)S(1)} %copy-done), kind=kOutput, calls=%fused_computation.54 | convolution fusion | flops 1610612736 | bytes 8388608 | tf_op jit(solution)/shard_map/ksd,kfd->ksf/dot_general | solution.py:51
  73.8 1.8 %fusion.3 = f32[2,512,768]{2,1,0:T(8,128)S(1)} fusion(bf16[2,512,1024]{2,1,0:T(8,128)(2,1)S(1)} %bitcast.36, bf16[2,1024,1536]{2,1,0:T(8,128)(2,1)S(1)} %bitcast.49), kind=kOutput, calls=%fused_computation.13 | convolution fusion | flops 1610612736 | bytes 8388608 | tf_op jit(solution)/shard_map/ksd,kdf->ksf/dot_general | solution.py:13
  75.6 3.0 %multiply_convert_fusion.2 = (bf16[2,512,768]{2,1,0:T(8,128)(2,1)S(1)}, bf16[2,512,768]{2,1,0:T(8,128)(2,1)S(1)}, f32[2,512,768]{2,1,0:T(8,128)S(1)}) fusion(f32[2,512,768]{2,1,0:T(8,128)S(1)} %fusion.32, f32[2,512,768]{2,1,0:T(8,128)S(1)} %fusion.3, bf16[2,512,1024]{2,1,0:T(8,128)(2,1)S(1)} %bitcast.37, bf16[2,1024,1536]{2,1,0:T(8,128)(2,1)S(1)} %bitcast.49), kind=kOutput, calls=%fused_computation.8 | convolution fusion | flops 1620836352 | bytes 17825792 | tf_op jit(solution)/shard_map/ksd,kdf->ksf/dot_general | solution.py:10
  78.6 2.0 %convolution_convert_fusion.1 = bf16[2,768,1024]{2,1,0:T(8,128)(2,1)S(1)} fusion(bf16[2,512,1024]{2,1,0:T(8,128)(2,1)S(1)} %bitcast.40, f32[2,512,768]{2,1,0:T(8,128)S(1)} %fusion.3, f32[2,512,768]{2,1,0:T(8,128)S(1)} %get-tuple-element.17), kind=kOutput, calls=%fused_computation.15 | convolution fusion | flops 1616904192 | bytes 11534336 | tf_op jit(solution)/shard_map/ksf,ksd->kfd/dot_general | solution.py:54
  81.0 3.8 %convolution_convert_fusion = bf16[2,1024,1536]{2,1,0:T(8,128)(2,1)S(1)} fusion(bf16[2,512,1024]{2,1,0:T(8,128)(2,1)S(1)} %bitcast.38, bf16[2,512,768]{2,1,0:T(8,128)(2,1)S(1)} %get-tuple-element.6, bf16[2,512,768]{2,1,0:T(8,128)(2,1)S(1)} %get-tuple-element.5), kind=kOutput, calls=%fused_computation.3 | convolution fusion | flops 3230662656 | bytes 11534336 | tf_op jit(solution)/shard_map/ksd,ksf->kdf/dot_general | solution.py:60
  84.8 4.1 %maximum_maximum_fusion = bf16[2,16,96,1536]{3,2,1,0:T(8,128)(2,1)} fusion(bf16[2,16,16,512]{3,2,1,0:T(8,128)(2,1)S(1)} %get-tuple-element.10, bf16[2,16,16,512]{3,2,1,0:T(8,128)(2,1)S(1)} %get-tuple-element.9, bf16[2,16,32,1024]{3,2,1,0:T(8,128)(2,1)S(1)} %slice.74, bf16[2,16,64,1536]{3,2,1,0:T(8,128)(2,1)S(1)} %bitcast.33), kind=kLoop, calls=%fused_computation.1 | loop fusion | flops 37748736 | bytes 18874368 | tf_op jit(solution)/shard_map/concatenate | solution.py:76
  88.8 7.2 %fusion.9 = bf16[2,512,1024]{2,1,0:T(8,128)(2,1)S(1)} fusion(bf16[2,1024,1536]{2,1,0:T(8,128)(2,1)} %param.12, bf16[2,512,768]{2,1,0:T(8,128)(2,1)} %copy-done.5, bf16[2,512,768]{2,1,0:T(8,128)(2,1)} %copy-done.4), kind=kOutput, calls=%fused_computation.24 | convolution fusion | flops 3228565504 | bytes 11534336 | tf_op jit(solution)/shard_map/ksf,kdf->ksd/dot_general | solution.py:61
  96.0 3.5 %copy.20 = bf16[2,512,1024]{2,0,1:T(2,128)(2,1)} copy(bf16[2,512,1024]{2,1,0:T(8,128)(2,1)S(1)} %fusion.9) | data formatting | bytes 4194304 | tf_op jit(solution)/shard_map/convert_element_type | solution.py:63
  99.5 6.2 %all-to-all-start.1 = ((bf16[2,512,1024]{2,0,1:T(2,128)(2,1)}), bf16[2,512,1024]{2,0,1:T(2,128)(2,1)S(1)}, u32[]{:S(2)}, u32[]{:S(2)}) async-start(bf16[2,512,1024]{2,0,1:T(2,128)(2,1)} %copy.20), calls=%async_computation.1 | async-start | bytes 4194304 | tf_op jit(solution)/shard_map/all_to_all | solution.py:64
  106.0 25.2 %all-to-all-done.1 = bf16[2,512,1024]{2,0,1:T(2,128)(2,1)S(1)} async-done(((bf16[2,512,1024]{2,0,1:T(2,128)(2,1)}), bf16[2,512,1024]{2,0,1:T(2,128)(2,1)S(1)}, u32[]{:S(2)}, u32[]{:S(2)}) %all-to-all-start.1) | async-done | bytes 2097184 | tf_op jit(solution)/shard_map/all_to_all | solution.py:64
  131.3 2.0 %copy.21 = bf16[2,16,32,1024]{3,2,0,1:T(8,128)(2,1)} copy(bf16[2,16,32,1024]{3,0,2,1:T(2,128)(2,1)S(1)} %bitcast.32) | data formatting | bytes 4194304 | tf_op jit(solution)/shard_map/all_to_all | solution.py:64
  133.3 5.5 %gather_fusion = bf16[512,1024]{1,0:T(8,128)(2,1)} fusion(bf16[1024,1024]{1,0:T(8,128)(2,1)} %bitcast.27, s32[1024]{0:T(1024)S(1)} %pad_clamp_fusion), kind=kCustom, calls=%fused_computation | custom fusion | bytes 2099200 | tf_op jit(solution)/shard_map/gather | solution.py:65
  138.8 2.3 %reshape.84 = bf16[256,2,1024]{2,1,0:T(2,128)(2,1)} reshape(bf16[512,1024]{1,0:T(8,128)(2,1)} %gather_fusion) | data formatting | bytes 2097152 | tf_op jit(solution)/shard_map/reshape | solution.py:65
  141.1 4.6 %reduce_sum.12 = bf16[256,1024]{1,0:T(8,128)(2,1)} reduce(bf16[256,2,1024]{2,1,0:T(2,128)(2,1)} %reshape.84, bf16[]{:T(256)} %constant.4.clone.1), dimensions={1}, to_apply=%region_0.0 | reduce | flops 262144 | bytes 1572866 | tf_op jit(solution)/shard_map/reduce_sum | solution.py:66
  145.7 17.9 %reduce-scatter.2.cloned.1.call-done = bf16[2,96,1536]{2,1,0:T(8,128)(2,1)} async-done(((bf16[2,1536,1536]{2,1,0:T(8,128)(2,1)}), bf16[2,96,1536]{2,1,0:T(8,128)(2,1)}) %reduce-scatter.2.cloned.1.call-update) | async-done | bytes 589840 | tf_op jit(solution)/shard_map/reduce_scatter | solution.py:77
  164.3 0.9 slice.78
  165.2 0.8 maximum_convert_fusion
  166.0 2.0 %slice_convert_fusion = f32[2,64,1536]{2,1,0:T(8,128)} fusion(bf16[2,96,1536]{2,1,0:T(8,128)(2,1)} %reduce-scatter.2.cloned.1.call-done), kind=kLoop, calls=%fused_computation.37 | loop fusion | flops 196608 | bytes 1179648 | tf_op jit(solution)/shard_map/convert_element_type | solution.py:78
  (31 shorter events, 2.5 us)
Async XLA Ops:
  7.2 64.2 %copy-start = (bf16[2,768,1024]{2,1,0:T(8,128)(2,1)S(1)}, bf16[2,768,1024]{2,1,0:T(8,128)(2,1)}, u32[]{:S(2)}) copy-start(bf16[2,768,1024]{2,1,0:T(8,128)(2,1)} %param.13) | copy-start | bytes 9437188
  7.2 156.4 %reduce-scatter.2.cloned.1.call-start = ((), (), s32[]{:S(2)}) async-start(), calls=%async_computation.3 | async-start | bytes 10027008 | tf_op jit(solution)/shard_map/reduce_scatter | solution.py:77
  8.1 2.4 %copy-start.3 = (f32[256,2]{0,1:T(2,128)S(1)}, f32[256,2]{0,1:T(2,128)}, u32[]{:S(2)}) copy-start(f32[256,2]{0,1:T(2,128)} %param.9) | copy-start | bytes 6148
  8.1 2.4 %copy-start.2 = (bf16[256,1024]{1,0:T(8,128)(2,1)S(1)}, bf16[256,1024]{1,0:T(8,128)(2,1)}, u32[]{:S(2)}) copy-start(bf16[256,1024]{1,0:T(8,128)(2,1)} %param.8) | copy-start | bytes 1572868
  70.8 2.5 %slice-start = ((s8[6291456]{0:T(1024)(128)(4,1)}), s8[2097152]{0:T(1024)(128)(4,1)S(1)}, s32[]{:S(2)}) async-start(s8[6291456]{0:T(1024)(128)(4,1)} %bitcast.48), calls=%async_computation.4 | async-start | bytes 4194304
  71.4 2.4 %slice-start.1 = ((s8[6291456]{0:T(1024)(128)(4,1)}), s8[4194304]{0:T(1024)(128)(4,1)S(1)}, s32[]{:S(2)}) async-start(s8[6291456]{0:T(1024)(128)(4,1)} %bitcast.48), calls=%async_computation.5 | async-start | bytes 8388608
  78.6 2.4 %copy-start.4 = (bf16[2,512,768]{2,1,0:T(8,128)(2,1)}, bf16[2,512,768]{2,1,0:T(8,128)(2,1)S(1)}, u32[]{:S(2)}) copy-start(bf16[2,512,768]{2,1,0:T(8,128)(2,1)S(1)} %get-tuple-element.5) | copy-start | bytes 4718596
  78.6 2.4 %copy-start.5 = (bf16[2,512,768]{2,1,0:T(8,128)(2,1)}, bf16[2,512,768]{2,1,0:T(8,128)(2,1)S(1)}, u32[]{:S(2)}) copy-start(bf16[2,512,768]{2,1,0:T(8,128)(2,1)S(1)} %get-tuple-element.6) | copy-start | bytes 4718596
  99.5 31.8 %all-to-all-start.1 = ((bf16[2,512,1024]{2,0,1:T(2,128)(2,1)}), bf16[2,512,1024]{2,0,1:T(2,128)(2,1)S(1)}, u32[]{:S(2)}, u32[]{:S(2)}) async-start(bf16[2,512,1024]{2,0,1:T(2,128)(2,1)} %copy.20), calls=%async_computation.1 | async-start | bytes 4194304 | tf_op jit(solution)/shard_map/all_to_all | solution.py:64
  133.3 34.7 %copy-start.1 = (bf16[2,768,1024]{2,1,0:T(8,128)(2,1)S(1)}, bf16[2,768,1024]{2,1,0:T(8,128)(2,1)}, u32[]{:S(2)}) copy-start(bf16[2,768,1024]{2,1,0:T(8,128)(2,1)} %param.13) | copy-start | bytes 9437188
Sparse Core Ops, SparseCore 0:
  88.9 74.5 reduce-scatter.1
where the time goes:
time: 175 us
  blocking collectives  55.5 us (32%)
  waiting for transfers between devices  43.1 us (25%)
  matrix products  26 us (15%)
  local copies, waits for them, and re-layouts  17.4 us (10%)
  between operations  14.3 us (8%)
  other arithmetic  12.3 us (7%)
  starting transfers between devices  6.27 us (4%)
    all_to_all x1, blocking collectives, per_device(): lax.all_to_all(send, 'expert', split_axis=0, concat_axis=0, tiled=True)  55.5 us
    all_to_all x1, waiting for transfers between devices, per_device(): lax.all_to_all(returned, 'expert', split_axis=1, concat_axis=0, tiled=True)  25.2 us
    reduce_scatter x1, waiting for transfers between devices, per_device(): summed = lax.psum_scatter(parts, 'dp', scatter_dimension=1, tiled=True)  17.9 us
    dot_general x1, matrix products, per_device(): jnp.einsum('ksf,kdf->ksd', grad_pair, w_in, preferred_element_type=jnp.fl...  7.19 us
    all_to_all x1, starting transfers between devices, per_device(): lax.all_to_all(returned, 'expert', split_axis=1, concat_axis=0, tiled=True)  6.23 us
    gather x1, local copies, waits for them, and re-layouts, per_device(): arrived.reshape(-1, width)[destination].reshape(token_count, TOP, width)  5.53 us
    reduce_sum x1, other arithmetic, per_device(): input_grad = jnp.sum(rows.astype(jnp.float32), axis=1).astype(jnp.bfloat16)  4.59 us
    concatenate x1, other arithmetic, per_device(): jnp.concatenate([part_in, packed], axis=2)  4.05 us
  transfers between devices with their start and end apart: 2, of which 2 were waited for; matrix products, arithmetic and copies ran while one was open for 14% of the time, Pallas kernels for 0%

commit v1 on v0

--- a/solution.py
+++ b/solution.py
@@ -4,6 +4,21 @@
 from jax.sharding import PartitionSpec as P
 
 TOP = 2
+
+
+def hold_the_digits(inp, on_dim, here_x):
+    now, s_next = (inp.shape[:on_dim], inp.shape[on_dim + 1 :])
+    big = jnp.moveaxis(inp.reshape(*now, here_x, -1, *s_next), on_dim, 0)
+    return big
+
+
+def handle_classes(incoming_x, along_dim):
+    incoming_x = jnp.moveaxis(incoming_x, 0, along_dim)
+    then = incoming_x.shape
+    v_now = incoming_x.reshape(
+        *then[:along_dim], then[along_dim] * then[along_dim + 1], *then[along_dim + 2 :]
+    )
+    return v_now
 
 
 def recompute(input_slots, w_in, hidden_width):
@@ -61,7 +76,18 @@
     returned = jnp.einsum(
         "ksf,kdf->ksd", grad_pair, w_in, preferred_element_type=jnp.float32
     ).astype(jnp.bfloat16)
-    arrived = lax.all_to_all(returned, "expert", split_axis=1, concat_axis=0, tiled=True)
+    step_out = jax.lax.psum(1, "expert")
+    answer = jax.lax.axis_index("expert")
+    arr_next, r1 = (step_out, answer)
+    shaped = hold_the_digits(returned, 1, arr_next)
+    vals = [shaped[r1]]
+    for nth in range(1, arr_next):
+        row_out = shaped[r1 ^ nth]
+        p_next = jax.lax.ppermute(row_out, "expert", [(kk, kk ^ nth) for kk in range(arr_next)])
+        vals.append(p_next)
+    outer = jnp.stack(vals, axis=0)
+    shaped = outer[r1 ^ jnp.arange(arr_next)]
+    arrived = handle_classes(shaped, 0)
     rows = arrived.reshape(-1, width)[destination].reshape(token_count, TOP, width)
     input_grad = jnp.sum(rows.astype(jnp.float32), axis=1).astype(jnp.bfloat16)
     in_rows, in_cols = (term_in.shape[1], term_in.shape[2])

time: 175 us -> 175 us (level)
  waiting for transfers between devices: 43.1 us -> 14.2 us
  starting transfers between devices: 6.27 us -> 28.1 us
  local copies, waits for them, and re-layouts: 17.4 us -> 23.9 us
    ppermute x0 -> x15, starting transfers between devices: none -> 28.1 us  [per_device(): jax.lax.ppermute(row_out, 'expert', [(kk, kk ^ nth) for kk in range(arr_n...]
    all_to_all x1 -> x0, waiting for transfers between devices: 25.2 us -> none  [per_device(): lax.all_to_all(returned, 'expert', split_axis=1, concat_axis=0, tiled=True)]
    unnamed x16 -> x31, local copies, waits for them, and re-layouts: 0.48 us -> 11.4 us
    reduce_scatter x1, waiting for transfers between devices: 17.9 us -> 10.6 us  [per_device(): summed = lax.psum_scatter(parts, 'dp', scatter_dimension=1, tiled=True)]
    all_to_all x1 -> x0, starting transfers between devices: 6.23 us -> none  [per_device(): lax.all_to_all(returned, 'expert', split_axis=1, concat_axis=0, tiled=True)]
    ppermute x0 -> x15, waiting for transfers between devices: none -> 3.61 us  [per_device(): jax.lax.ppermute(row_out, 'expert', [(kk, kk ^ nth) for kk in range(arr_n...]
    convert_element_type x1 -> x0, local copies, waits for them, and re-layouts: 3.47 us -> none  [per_device(): returned = jnp.einsum('ksf,kdf->ksd', grad_pair, w_in, preferred_element_...]
    gather x1, local copies, waits for them, and re-layouts: 5.53 us -> 2.81 us  [per_device(): arrived.reshape(-1, width)[destination].reshape(token_count, TOP, width)]
  transfers between devices with their start and end apart: 2 -> 16, of which waited for: 2 -> 3; matrix products, arithmetic and copies ran while one was open for 14% -> 18% of each run, Pallas kernels for 0% -> 0%
where the time goes in v1:
time: 175 us; the launch traced here: 174 us
  blocking collectives  55.5 us (32%)
  starting transfers between devices  28.1 us (16%)
  matrix products  26 us (15%)
  local copies, waits for them, and re-layouts  23.9 us (14%)
  between operations  14.4 us (8%)
  waiting for transfers between devices  14.2 us (8%)
  other arithmetic  12.3 us (7%)
    all_to_all x1, blocking collectives, per_device(): lax.all_to_all(send, 'expert', split_axis=0, concat_axis=0, tiled=True)  55.5 us
    ppermute x15, starting transfers between devices, per_device(): jax.lax.ppermute(row_out, 'expert', [(kk, kk ^ nth) for kk in range(arr_n...  28.1 us
    unnamed x31, local copies, waits for them, and re-layouts  11.4 us
    reduce_scatter x1, waiting for transfers between devices, per_device(): summed = lax.psum_scatter(parts, 'dp', scatter_dimension=1, tiled=True)  10.6 us
    dot_general x1, matrix products, per_device(): jnp.einsum('ksf,kdf->ksd', grad_pair, w_in, preferred_element_type=jnp.fl...  7.19 us
    reduce_sum x1, other arithmetic, per_device(): input_grad = jnp.sum(rows.astype(jnp.float32), axis=1).astype(jnp.bfloat16)  4.58 us
    concatenate x1, other arithmetic, per_device(): jnp.concatenate([part_in, packed], axis=2)  4.07 us
    dot_general x2, matrix products, per_device(): send = send + jnp.dot(shifted, scaled, preferred_element_type=jnp.float32)  3.95 us
  transfers between devices with their start and end apart: 16, of which 3 were waited for; matrix products, arithmetic and copies ran while one was open for 18% of the time, Pallas kernels for 0%

profile of v1, /device:TPU:4, one launch (start us, length us, event | category | flops | bytes accessed | tf_op | source)
XLA Modules:
  0.0 174.5 jit_solution(10992559125790744478)
XLA Ops:
  8.1 2.4 %fusion.13 = f32[2048,1024]{1,0:T(8,128)S(1)} fusion(bf16[256,1024]{1,0:T(8,128)(2,1)} %param.7, s32[256]{0:T(256)S(1)} %bitcast.107, s32[256]{0:T(256)S(1)} %bitcast.105), kind=kOutput, calls=%fused_computation.31 | convolution fusion | flops 1077936128 | bytes 8914944 | tf_op jit(solution)/shard_map/dot_general | solution.py:55
  11.9 2.6 %add_convert_fusion = bf16[2048,1024]{1,0:T(8,128)(2,1)S(1)} fusion(f32[2048,1024]{1,0:T(8,128)S(1)} %fusion.13, f32[2048,1024]{1,0:T(8,128)S(1)} %fusion.7, s32[256]{0:T(256)S(1)} %broadcast_add_fusion, bf16[256,1024]{1,0:T(8,128)(2,1)} %param.8, f32[256]{0:T(256)S(1)} %bitcast.109), kind=kOutput, calls=%fused_computation.3 | convolution fusion | flops 1081344000 | bytes 21497856 | tf_op jit(solution)/shard_map/dot_general | solution.py:59
  14.5 55.5 %all_to_all.5 = bf16[32,2,32,1024]{3,2,1,0:T(8,128)(2,1)S(1)} all-to-all(bf16[32,2,32,1024]{3,2,1,0:T(8,128)(2,1)S(1)} %bitcast.93), channel_id=1, replica_groups=mesh['dp'=16,'expert'=16] {'expert'}, dimensions={0} | all-to-all | bytes 8388608 | tf_op jit(solution)/shard_map/all_to_all | solution.py:61
  71.1 1.9 %fusion.33 = f32[2,512,768]{2,1,0:T(8,128)S(1)} fusion(bf16[2,512,1024]{2,1,0:T(8,128)(2,1)S(1)} %bitcast.102, bf16[2,768,1024]{2,1,0:T(8,128)(2,1)S(1)} %copy-done), kind=kOutput, calls=%fused_computation.89 | convolution fusion | flops 1610612736 | bytes 8388608 | tf_op jit(solution)/shard_map/ksd,kfd->ksf/dot_general | solution.py:66
  73.4 1.8 %fusion.3 = f32[2,512,768]{2,1,0:T(8,128)S(1)} fusion(bf16[2,512,1024]{2,1,0:T(8,128)(2,1)S(1)} %bitcast.99, bf16[2,1024,1536]{2,1,0:T(8,128)(2,1)S(1)} %bitcast.112), kind=kOutput, calls=%fused_computation.14 | convolution fusion | flops 1610612736 | bytes 8388608 | tf_op jit(solution)/shard_map/ksd,kdf->ksf/dot_general | solution.py:28
  75.2 3.0 %multiply_convert_fusion.2 = (bf16[2,512,768]{2,1,0:T(8,128)(2,1)S(1)}, bf16[2,512,768]{2,1,0:T(8,128)(2,1)S(1)}, f32[2,512,768]{2,1,0:T(8,128)S(1)}) fusion(f32[2,512,768]{2,1,0:T(8,128)S(1)} %fusion.33, f32[2,512,768]{2,1,0:T(8,128)S(1)} %fusion.3, bf16[2,512,1024]{2,1,0:T(8,128)(2,1)S(1)} %bitcast.100, bf16[2,1024,1536]{2,1,0:T(8,128)(2,1)S(1)} %bitcast.112), kind=kOutput, calls=%fused_computation.9 | convolution fusion | flops 1620836352 | bytes 17825792 | tf_op jit(solution)/shard_map/ksd,kdf->ksf/dot_general | solution.py:25
  78.3 2.1 %convolution_convert_fusion.1 = bf16[2,768,1024]{2,1,0:T(8,128)(2,1)S(1)} fusion(bf16[2,512,1024]{2,1,0:T(8,128)(2,1)S(1)} %bitcast.103, f32[2,512,768]{2,1,0:T(8,128)S(1)} %fusion.3, f32[2,512,768]{2,1,0:T(8,128)S(1)} %get-tuple-element.32), kind=kOutput, calls=%fused_computation.16 | convolution fusion | flops 1616904192 | bytes 11534336 | tf_op jit(solution)/shard_map/ksf,ksd->kfd/dot_general | solution.py:69
  80.7 3.8 %convolution_convert_fusion = bf16[2,1024,1536]{2,1,0:T(8,128)(2,1)S(1)} fusion(bf16[2,512,1024]{2,1,0:T(8,128)(2,1)S(1)} %bitcast.101, bf16[2,512,768]{2,1,0:T(8,128)(2,1)S(1)} %get-tuple-element.6, bf16[2,512,768]{2,1,0:T(8,128)(2,1)S(1)} %get-tuple-element.5), kind=kOutput, calls=%fused_computation.4 | convolution fusion | flops 3230662656 | bytes 11534336 | tf_op jit(solution)/shard_map/ksd,ksf->kdf/dot_general | solution.py:75
  84.5 4.1 %maximum_maximum_fusion = bf16[2,16,96,1536]{3,2,1,0:T(8,128)(2,1)} fusion(bf16[2,16,16,512]{3,2,1,0:T(8,128)(2,1)S(1)} %get-tuple-element.10, bf16[2,16,16,512]{3,2,1,0:T(8,128)(2,1)S(1)} %get-tuple-element.9, bf16[2,16,32,1024]{3,2,1,0:T(8,128)(2,1)S(1)} %slice.76, bf16[2,16,64,1536]{3,2,1,0:T(8,128)(2,1)S(1)} %bitcast.94), kind=kLoop, calls=%fused_computation.2 | loop fusion | flops 37748736 | bytes 18874368 | tf_op jit(solution)/shard_map/concatenate | solution.py:102
  89.0 7.2 %fusion.9 = bf16[2,512,1024]{2,1,0:T(8,128)(2,1)S(1)} fusion(bf16[2,1024,1536]{2,1,0:T(8,128)(2,1)} %param.12, bf16[2,512,768]{2,1,0:T(8,128)(2,1)} %copy-done.5, bf16[2,512,768]{2,1,0:T(8,128)(2,1)} %copy-done.4), kind=kOutput, calls=%fused_computation.25 | convolution fusion | flops 3228565504 | bytes 11534336 | tf_op jit(solution)/shard_map/ksf,kdf->ksd/dot_general | solution.py:76
  98.4 2.1 %collective-permute-start.1 = (bf16[2,32,1024]{2,1,0:T(8,128)(2,1)}, bf16[2,32,1024]{2,1,0:T(8,128)(2,1)S(1)}, u32[]{:S(2)}, u32[]{:S(2)}) collective-permute-start(bf16[2,32,1024]{2,1,0:T(8,128)(2,1)} %get-tuple-element.24), channel_id=1, source_target_pairs={{0,2},{1,3},{2,0},{3,1},{4,6},{5,7},{6,4},{7,5},{8,10},{9,11},{10,... | collective-permute-start | bytes 393224 | tf_op jit(solution)/shard_map/ppermute | solution.py:86
  101.4 3.2 %collective-permute-start.4 = (bf16[2,32,1024]{2,1,0:T(8,128)(2,1)S(1)}, bf16[2,32,1024]{2,1,0:T(8,128)(2,1)S(1)}, u32[]{:S(2)}, u32[]{:S(2)}) collective-permute-start(bf16[2,32,1024]{2,1,0:T(8,128)(2,1)S(1)} %get-tuple-element.21), channel_id=1, source_target_pairs={{0,5},{1,4},{2,7},{3,6},{4,1},{5,0},{6,3},{7,2},{8,13},{9,12},{10,... | collective-permute-start | bytes 393224 | tf_op jit(solution)/shard_map/ppermute | solution.py:86
  106.8 1.6 bitcast_dynamic-update-slice_fusion.14
  109.5 1.9 %collective-permute-start.7 = (bf16[2,32,1024]{2,1,0:T(8,128)(2,1)S(1)}, bf16[2,32,1024]{2,1,0:T(8,128)(2,1)S(1)}, u32[]{:S(2)}, u32[]{:S(2)}) collective-permute-start(bf16[2,32,1024]{2,1,0:T(8,128)(2,1)S(1)} %get-tuple-element.18), channel_id=1, source_target_pairs={{0,8},{1,9},{2,10},{3,11},{4,12},{5,13},{6,14},{7,15},{8,0},{9,1},... | collective-permute-start | bytes 393224 | tf_op jit(solution)/shard_map/ppermute | solution.py:86
  112.0 4.7 %collective-permute-start.8 = (bf16[2,32,1024]{2,1,0:T(8,128)(2,1)S(1)}, bf16[2,32,1024]{2,1,0:T(8,128)(2,1)S(1)}, u32[]{:S(2)}, u32[]{:S(2)}) collective-permute-start(bf16[2,32,1024]{2,1,0:T(8,128)(2,1)S(1)} %get-tuple-element.17), channel_id=1, source_target_pairs={{0,9},{1,8},{2,11},{3,10},{4,13},{5,12},{6,15},{7,14},{8,1},{9,0},... | collective-permute-start | bytes 393224 | tf_op jit(solution)/shard_map/ppermute | solution.py:86
  121.2 1.8 %collective-permute-start.11 = (bf16[2,32,1024]{2,1,0:T(8,128)(2,1)S(1)}, bf16[2,32,1024]{2,1,0:T(8,128)(2,1)S(1)}, u32[]{:S(2)}, u32[]{:S(2)}) collective-permute-start(bf16[2,32,1024]{2,1,0:T(8,128)(2,1)S(1)} %get-tuple-element.14), channel_id=1, source_target_pairs={{0,12},{1,13},{2,14},{3,15},{4,8},{5,9},{6,10},{7,11},{8,4},{9,5},... | collective-permute-start | bytes 393224 | tf_op jit(solution)/shard_map/ppermute | solution.py:86
  123.6 5.5 %collective-permute-start.12 = (bf16[2,32,1024]{2,1,0:T(8,128)(2,1)S(1)}, bf16[2,32,1024]{2,1,0:T(8,128)(2,1)S(1)}, u32[]{:S(2)}, u32[]{:S(2)}) collective-permute-start(bf16[2,32,1024]{2,1,0:T(8,128)(2,1)S(1)} %get-tuple-element.13), channel_id=1, source_target_pairs={{0,13},{1,12},{2,15},{3,14},{4,9},{5,8},{6,11},{7,10},{8,5},{9,4},... | collective-permute-start | bytes 393224 | tf_op jit(solution)/shard_map/ppermute | solution.py:86
  135.6 2.9 %collective-permute-done.13 = bf16[2,32,1024]{2,1,0:T(8,128)(2,1)S(1)} collective-permute-done((bf16[2,32,1024]{2,1,0:T(8,128)(2,1)S(1)}, bf16[2,32,1024]{2,1,0:T(8,128)(2,1)S(1)}, u32[]{:S(2)}, u32[]{:S(2)}) %collective-permute-start.13) | collective-permute-done | bytes 131104 | tf_op jit(solution)/shard_map/ppermute | solution.py:86
  140.5 2.3 %gather_fusion = bf16[16,2,32,1024]{3,2,1,0:T(8,128)(2,1)S(1)} fusion(bf16[16,2,32,1024]{3,2,1,0:T(8,128)(2,1)} %bitcast_dynamic-update-slice_fusion, s32[1024]{0:T(1024)S(1)} %pad_clamp_fusion.1), kind=kCustom, calls=%fused_computation | custom fusion | bytes 4194368 | tf_op jit(solution)/shard_map/gather | solution.py:89
  142.8 2.8 %gather_fusion.1 = bf16[512,1024]{1,0:T(8,128)(2,1)} fusion(bf16[1024,1024]{1,0:T(8,128)(2,1)S(1)} %bitcast.89, s32[1024]{0:T(1024)S(1)} %pad_clamp_fusion), kind=kCustom, calls=%fused_computation.1 | custom fusion | bytes 2099200 | tf_op jit(solution)/shard_map/gather | solution.py:91
  145.6 2.4 %reshape.130 = bf16[256,2,1024]{2,1,0:T(2,128)(2,1)} reshape(bf16[512,1024]{1,0:T(8,128)(2,1)} %gather_fusion.1) | data formatting | bytes 2097152 | tf_op jit(solution)/shard_map/reshape | solution.py:91
  148.0 4.6 %reduce_sum.12 = bf16[256,1024]{1,0:T(8,128)(2,1)} reduce(bf16[256,2,1024]{2,1,0:T(2,128)(2,1)} %reshape.130, bf16[]{:T(256)} %constant.18.clone.1), dimensions={1}, to_apply=%region_0.0 | reduce | flops 262144 | bytes 1572866 | tf_op jit(solution)/shard_map/reduce_sum | solution.py:92
  152.6 10.6 %reduce-scatter.2.cloned.1.call-done = bf16[2,96,1536]{2,1,0:T(8,128)(2,1)} async-done(((bf16[2,1536,1536]{2,1,0:T(8,128)(2,1)}), bf16[2,96,1536]{2,1,0:T(8,128)(2,1)}) %reduce-scatter.2.cloned.1.call-update) | async-done | bytes 589840 | tf_op jit(solution)/shard_map/reduce_scatter | solution.py:103
  165.7 2.0 %slice_convert_fusion = f32[2,64,1536]{2,1,0:T(8,128)} fusion(bf16[2,96,1536]{2,1,0:T(8,128)(2,1)} %reduce-scatter.2.cloned.1.call-done), kind=kLoop, calls=%fused_computation.38 | loop fusion | flops 196608 | bytes 1179648 | tf_op jit(solution)/shard_map/convert_element_type | solution.py:104
  (77 shorter events, 27.5 us)
Async XLA Ops:
  7.2 63.9 %copy-start = (bf16[2,768,1024]{2,1,0:T(8,128)(2,1)S(1)}, bf16[2,768,1024]{2,1,0:T(8,128)(2,1)}, u32[]{:S(2)}) copy-start(bf16[2,768,1024]{2,1,0:T(8,128)(2,1)} %param.13) | copy-start | bytes 9437188
  7.2 156.0 %reduce-scatter.2.cloned.1.call-start = ((), (), s32[]{:S(2)}) async-start(), calls=%async_computation.2 | async-start | bytes 10027008 | tf_op jit(solution)/shard_map/reduce_scatter | solution.py:103
  8.1 2.4 %copy-start.3 = (f32[256,2]{0,1:T(2,128)S(1)}, f32[256,2]{0,1:T(2,128)}, u32[]{:S(2)}) copy-start(f32[256,2]{0,1:T(2,128)} %param.9) | copy-start | bytes 6148
  8.1 2.4 %copy-start.2 = (bf16[256,1024]{1,0:T(8,128)(2,1)S(1)}, bf16[256,1024]{1,0:T(8,128)(2,1)}, u32[]{:S(2)}) copy-start(bf16[256,1024]{1,0:T(8,128)(2,1)} %param.8) | copy-start | bytes 1572868
  70.4 2.5 %slice-start = ((s8[6291456]{0:T(1024)(128)(4,1)}), s8[4194304]{0:T(1024)(128)(4,1)S(1)}, s32[]{:S(2)}) async-start(s8[6291456]{0:T(1024)(128)(4,1)} %bitcast.111), calls=%async_computation.3 | async-start | bytes 8388608
  71.0 2.4 %slice-start.1 = ((s8[6291456]{0:T(1024)(128)(4,1)}), s8[2097152]{0:T(1024)(128)(4,1)S(1)}, s32[]{:S(2)}) async-start(s8[6291456]{0:T(1024)(128)(4,1)} %bitcast.111), calls=%async_computation.4 | async-start | bytes 4194304
  78.2 2.4 %copy-start.4 = (bf16[2,512,768]{2,1,0:T(8,128)(2,1)}, bf16[2,512,768]{2,1,0:T(8,128)(2,1)S(1)}, u32[]{:S(2)}) copy-start(bf16[2,512,768]{2,1,0:T(8,128)(2,1)S(1)} %get-tuple-element.5) | copy-start | bytes 4718596
  78.2 2.4 %copy-start.5 = (bf16[2,512,768]{2,1,0:T(8,128)(2,1)}, bf16[2,512,768]{2,1,0:T(8,128)(2,1)S(1)}, u32[]{:S(2)}) copy-start(bf16[2,512,768]{2,1,0:T(8,128)(2,1)S(1)} %get-tuple-element.6) | copy-start | bytes 4718596
  97.3 8.0 %collective-permute-start = (bf16[2,32,1024]{2,1,0:T(8,128)(2,1)}, bf16[2,32,1024]{2,1,0:T(8,128)(2,1)}, u32[]{:S(2)}, u32[]{:S(2)}) collective-permute-start(bf16[2,32,1024]{2,1,0:T(8,128)(2,1)} %get-tuple-element.25), channel_id=1, source_target_pairs={{0,1},{1,0},{2,3},{3,2},{4,5},{5,4},{6,7},{7,6},{8,9},{9,8},{10,11... | collective-permute-start | bytes 393224 | tf_op jit(solution)/shard_map/ppermute | solution.py:86
  98.4 9.9 %collective-permute-start.1 = (bf16[2,32,1024]{2,1,0:T(8,128)(2,1)}, bf16[2,32,1024]{2,1,0:T(8,128)(2,1)S(1)}, u32[]{:S(2)}, u32[]{:S(2)}) collective-permute-start(bf16[2,32,1024]{2,1,0:T(8,128)(2,1)} %get-tuple-element.24), channel_id=1, source_target_pairs={{0,2},{1,3},{2,0},{3,1},{4,6},{5,7},{6,4},{7,5},{8,10},{9,11},{10,... | collective-permute-start | bytes 393224 | tf_op jit(solution)/shard_map/ppermute | solution.py:86
  100.6 8.9 %collective-permute-start.2 = (bf16[2,32,1024]{2,1,0:T(8,128)(2,1)}, bf16[2,32,1024]{2,1,0:T(8,128)(2,1)S(1)}, u32[]{:S(2)}, u32[]{:S(2)}) collective-permute-start(bf16[2,32,1024]{2,1,0:T(8,128)(2,1)} %get-tuple-element.23), channel_id=1, source_target_pairs={{0,3},{1,2},{2,1},{3,0},{4,7},{5,6},{6,5},{7,4},{8,11},{9,10},{10,... | collective-permute-start | bytes 393224 | tf_op jit(solution)/shard_map/ppermute | solution.py:86
  100.8 11.3 %collective-permute-start.3 = (bf16[2,32,1024]{2,1,0:T(8,128)(2,1)}, bf16[2,32,1024]{2,1,0:T(8,128)(2,1)S(1)}, u32[]{:S(2)}, u32[]{:S(2)}) collective-permute-start(bf16[2,32,1024]{2,1,0:T(8,128)(2,1)} %get-tuple-element.22), channel_id=1, source_target_pairs={{0,4},{1,5},{2,6},{3,7},{4,0},{5,1},{6,2},{7,3},{8,12},{9,13},{10,... | collective-permute-start | bytes 393224 | tf_op jit(solution)/shard_map/ppermute | solution.py:86
  101.4 16.0 %collective-permute-start.4 = (bf16[2,32,1024]{2,1,0:T(8,128)(2,1)S(1)}, bf16[2,32,1024]{2,1,0:T(8,128)(2,1)S(1)}, u32[]{:S(2)}, u32[]{:S(2)}) collective-permute-start(bf16[2,32,1024]{2,1,0:T(8,128)(2,1)S(1)} %get-tuple-element.21), channel_id=1, source_target_pairs={{0,5},{1,4},{2,7},{3,6},{4,1},{5,0},{6,3},{7,2},{8,13},{9,12},{10,... | collective-permute-start | bytes 393224 | tf_op jit(solution)/shard_map/ppermute | solution.py:86
  105.3 14.4 %collective-permute-start.5 = (bf16[2,32,1024]{2,1,0:T(8,128)(2,1)S(1)}, bf16[2,32,1024]{2,1,0:T(8,128)(2,1)S(1)}, u32[]{:S(2)}, u32[]{:S(2)}) collective-permute-start(bf16[2,32,1024]{2,1,0:T(8,128)(2,1)S(1)} %get-tuple-element.20), channel_id=1, source_target_pairs={{0,6},{1,7},{2,4},{3,5},{4,2},{5,3},{6,0},{7,1},{8,14},{9,15},{10,... | collective-permute-start | bytes 393224 | tf_op jit(solution)/shard_map/ppermute | solution.py:86
  108.4 12.8 %collective-permute-start.6 = (bf16[2,32,1024]{2,1,0:T(8,128)(2,1)S(1)}, bf16[2,32,1024]{2,1,0:T(8,128)(2,1)S(1)}, u32[]{:S(2)}, u32[]{:S(2)}) collective-permute-start(bf16[2,32,1024]{2,1,0:T(8,128)(2,1)S(1)} %get-tuple-element.19), channel_id=1, source_target_pairs={{0,7},{1,6},{2,5},{3,4},{4,3},{5,2},{6,1},{7,0},{8,15},{9,14},{10,... | collective-permute-start | bytes 393224 | tf_op jit(solution)/shard_map/ppermute | solution.py:86
  109.5 14.1 %collective-permute-start.7 = (bf16[2,32,1024]{2,1,0:T(8,128)(2,1)S(1)}, bf16[2,32,1024]{2,1,0:T(8,128)(2,1)S(1)}, u32[]{:S(2)}, u32[]{:S(2)}) collective-permute-start(bf16[2,32,1024]{2,1,0:T(8,128)(2,1)S(1)} %get-tuple-element.18), channel_id=1, source_target_pairs={{0,8},{1,9},{2,10},{3,11},{4,12},{5,13},{6,14},{7,15},{8,0},{9,1},... | collective-permute-start | bytes 393224 | tf_op jit(solution)/shard_map/ppermute | solution.py:86
  112.0 17.8 %collective-permute-start.8 = (bf16[2,32,1024]{2,1,0:T(8,128)(2,1)S(1)}, bf16[2,32,1024]{2,1,0:T(8,128)(2,1)S(1)}, u32[]{:S(2)}, u32[]{:S(2)}) collective-permute-start(bf16[2,32,1024]{2,1,0:T(8,128)(2,1)S(1)} %get-tuple-element.17), channel_id=1, source_target_pairs={{0,9},{1,8},{2,11},{3,10},{4,13},{5,12},{6,15},{7,14},{8,1},{9,0},... | collective-permute-start | bytes 393224 | tf_op jit(solution)/shard_map/ppermute | solution.py:86
  117.4 14.7 %collective-permute-start.9 = (bf16[2,32,1024]{2,1,0:T(8,128)(2,1)S(1)}, bf16[2,32,1024]{2,1,0:T(8,128)(2,1)S(1)}, u32[]{:S(2)}, u32[]{:S(2)}) collective-permute-start(bf16[2,32,1024]{2,1,0:T(8,128)(2,1)S(1)} %get-tuple-element.16), channel_id=1, source_target_pairs={{0,10},{1,11},{2,8},{3,9},{4,14},{5,15},{6,12},{7,13},{8,2},{9,3},... | collective-permute-start | bytes 393224 | tf_op jit(solution)/shard_map/ppermute | solution.py:86
  119.6 14.0 %collective-permute-start.10 = (bf16[2,32,1024]{2,1,0:T(8,128)(2,1)S(1)}, bf16[2,32,1024]{2,1,0:T(8,128)(2,1)S(1)}, u32[]{:S(2)}, u32[]{:S(2)}) collective-permute-start(bf16[2,32,1024]{2,1,0:T(8,128)(2,1)S(1)} %get-tuple-element.15), channel_id=1, source_target_pairs={{0,11},{1,10},{2,9},{3,8},{4,15},{5,14},{6,13},{7,12},{8,3},{9,2},... | collective-permute-start | bytes 393224 | tf_op jit(solution)/shard_map/ppermute | solution.py:86
  121.2 13.1 %collective-permute-start.11 = (bf16[2,32,1024]{2,1,0:T(8,128)(2,1)S(1)}, bf16[2,32,1024]{2,1,0:T(8,128)(2,1)S(1)}, u32[]{:S(2)}, u32[]{:S(2)}) collective-permute-start(bf16[2,32,1024]{2,1,0:T(8,128)(2,1)S(1)} %get-tuple-element.14), channel_id=1, source_target_pairs={{0,12},{1,13},{2,14},{3,15},{4,8},{5,9},{6,10},{7,11},{8,4},{9,5},... | collective-permute-start | bytes 393224 | tf_op jit(solution)/shard_map/ppermute | solution.py:86
  123.6 11.3 %collective-permute-start.12 = (bf16[2,32,1024]{2,1,0:T(8,128)(2,1)S(1)}, bf16[2,32,1024]{2,1,0:T(8,128)(2,1)S(1)}, u32[]{:S(2)}, u32[]{:S(2)}) collective-permute-start(bf16[2,32,1024]{2,1,0:T(8,128)(2,1)S(1)} %get-tuple-element.13), channel_id=1, source_target_pairs={{0,13},{1,12},{2,15},{3,14},{4,9},{5,8},{6,11},{7,10},{8,5},{9,4},... | collective-permute-start | bytes 393224 | tf_op jit(solution)/shard_map/ppermute | solution.py:86
  129.8 8.7 %collective-permute-start.13 = (bf16[2,32,1024]{2,1,0:T(8,128)(2,1)S(1)}, bf16[2,32,1024]{2,1,0:T(8,128)(2,1)S(1)}, u32[]{:S(2)}, u32[]{:S(2)}) collective-permute-start(bf16[2,32,1024]{2,1,0:T(8,128)(2,1)S(1)} %get-tuple-element.12), channel_id=1, source_target_pairs={{0,14},{1,15},{2,12},{3,13},{4,10},{5,11},{6,8},{7,9},{8,6},{9,7},... | collective-permute-start | bytes 393224 | tf_op jit(solution)/shard_map/ppermute | solution.py:86
  132.1 7.8 %collective-permute-start.14 = (bf16[2,32,1024]{2,1,0:T(8,128)(2,1)S(1)}, bf16[2,32,1024]{2,1,0:T(8,128)(2,1)S(1)}, u32[]{:S(2)}, u32[]{:S(2)}) collective-permute-start(bf16[2,32,1024]{2,1,0:T(8,128)(2,1)S(1)} %get-tuple-element.11), channel_id=1, source_target_pairs={{0,15},{1,14},{2,13},{3,12},{4,11},{5,10},{6,9},{7,8},{8,7},{9,6},... | collective-permute-start | bytes 393224 | tf_op jit(solution)/shard_map/ppermute | solution.py:86
  145.6 22.0 %copy-start.1 = (bf16[2,768,1024]{2,1,0:T(8,128)(2,1)S(1)}, bf16[2,768,1024]{2,1,0:T(8,128)(2,1)}, u32[]{:S(2)}) copy-start(bf16[2,768,1024]{2,1,0:T(8,128)(2,1)} %param.13) | copy-start | bytes 9437188
Sparse Core Ops, SparseCore 0:
  88.7 74.4 reduce-scatter.1
